TPU v7x, 256 devices: a whole 4x4x8 slice. The times are simulated.
256 devices in a mesh: dp: 4 (over y), expert: 64 (over x, z, core).
Axes of the slice: x: 4, y: 4, z: 8, core: 2. Of those that a mesh axis runs over, the one named last changes fastest.
Arguments:
- tokens: bfloat16 [6144, 4096], P(('dp', 'expert')), may hold values from -6 to 6
- out_grad: bfloat16 [6144, 4096], P(('dp', 'expert')), may hold values from -6 to 6
- routes: int32 [6144, 8], P(('dp', 'expert')), may hold values from 0 to 63, all different within a row; in each aligned block of 24 rows (0 to 23, 24 to 47, ...) at most 4 rows name the same one
- gates: bfloat16 [6144, 8], P(('dp', 'expert')), may hold values from 0.099609375 to 0.5
- w_gate: bfloat16 [64, 768, 4096], P('expert', 'dp'), may hold values from -0.09375 to 0.09375
- w_up: bfloat16 [64, 768, 4096], P('expert', 'dp'), may hold values from -0.09375 to 0.09375
- w_down: bfloat16 [64, 768, 4096], P('expert', 'dp'), may hold values from -0.21875 to 0.21875
Outputs:
- d_tokens: bfloat16 [6144, 4096], P(('dp', 'expert'))
- d_gate: bfloat16 [64, 768, 4096], P('expert', 'dp')
- d_up: bfloat16 [64, 768, 4096], P('expert', 'dp')
- d_down: bfloat16 [64, 768, 4096], P('expert', 'dp')
Inputs may be any that keep to these rules, and one draw needn't show every extreme that they name: `routes`: each row names 8 different experts. Within the 24 rows of one device no expert is named by more than 4 rows, and in every draw some expert is named by exactly 4 rows of some device.
All inputs are finite; a program needn't handle non-finite values.
Results may differ from a plain program's by a relative error of at most 0.015.
Values may be sent and summed in bfloat16 or wider, within the bound.
A program may use at most 128 MiB of HBM per device.

v0:
```python
from functools import partial
import jax
import jax.numpy as jnp
from jax import lax
from jax.sharding import PartitionSpec as P


def cell_match(routes, experts, capacity):
    expert_ids = jnp.arange(experts, dtype=jnp.int32)
    onehot = (routes[:, :, None] == expert_ids).astype(jnp.int32)
    chosen = jnp.sum(onehot, axis=1)
    earlier = jnp.cumsum(chosen, axis=0) - chosen
    slot_index = jnp.sum(onehot * earlier[:, None, :], axis=2)
    target = routes * capacity + slot_index
    cell_ids = jnp.arange(experts * capacity, dtype=jnp.int32)
    return target[:, :, None] == cell_ids


def placement(matches, experts, capacity):
    return jnp.any(matches, axis=1).reshape(-1, experts, capacity).astype(jnp.bfloat16)


def weighting(matches, gates, experts, capacity):
    spread = jnp.where(matches, gates.astype(jnp.float32)[:, :, None], 0.0)
    return jnp.sum(spread, axis=1).reshape(-1, experts, capacity)


def per_device(tokens, out_grad, routes, gates, w_gate, w_up, w_down):
    tok_rows, features = tokens.shape
    top_count = routes.shape[1]
    experts = lax.axis_size("expert")
    groups = lax.axis_size("dp")
    capacity = max(2, min(tok_rows, 3 * tok_rows * top_count // (2 * experts)))
    match_fn = partial(cell_match, experts=experts, capacity=capacity)
    place_fn = partial(placement, experts=experts, capacity=capacity)
    weight_fn = partial(weighting, experts=experts, capacity=capacity)
    own_match = match_fn(routes)
    own_place = place_fn(own_match)
    own_weight = weight_fn(own_match, gates)
    input_send = jnp.einsum(
        "tec,td->ecd", own_place, tokens, preferred_element_type=jnp.float32
    ).astype(jnp.bfloat16)
    grad_send = jnp.einsum(
        "tec,td->ecd", own_weight, out_grad.astype(jnp.float32), precision=lax.Precision.HIGHEST
    ).astype(jnp.bfloat16)
    input_recv, grad_recv = (
        lax.all_to_all(input_send, "expert", split_axis=0, concat_axis=0, tiled=True),
        lax.all_to_all(grad_send, "expert", split_axis=0, concat_axis=0, tiled=True),
    )
    input_recv = input_recv.reshape(experts, 1, capacity, features)
    grad_recv = grad_recv.reshape(experts, 1, capacity, features)
    input_slots, grad_slots = (
        lax.all_gather(input_recv, "dp", axis=1, tiled=True),
        lax.all_gather(grad_recv, "dp", axis=1, tiled=True),
    )
    input_rows = input_slots.reshape(-1, features)
    grad_rows = grad_slots.reshape(-1, features)
    gate_w = w_gate[0]
    up_w = w_up[0]
    down_w = w_down[0]
    gate_pre = jnp.einsum("rd,fd->rf", input_rows, gate_w, preferred_element_type=jnp.float32)
    up_pre = jnp.einsum("rd,fd->rf", input_rows, up_w, preferred_element_type=jnp.float32)
    sigmoid_gate = jax.nn.sigmoid(gate_pre)
    silu_gate = gate_pre * sigmoid_gate
    hidden = (silu_gate * up_pre).astype(jnp.bfloat16)
    d_hidden = jnp.einsum("rd,fd->rf", grad_rows, down_w, preferred_element_type=jnp.float32)
    d_up_act = (d_hidden * silu_gate).astype(jnp.bfloat16)
    d_gate_act = (
        d_hidden * up_pre * sigmoid_gate * (1.0 + gate_pre * (1.0 - sigmoid_gate))
    ).astype(jnp.bfloat16)
    grad_down = jnp.einsum(
        "rf,rd->fd", hidden, grad_rows, preferred_element_type=jnp.float32
    ).astype(jnp.bfloat16)
    grad_gate = jnp.einsum(
        "rf,rd->fd", d_gate_act, input_rows, preferred_element_type=jnp.float32
    ).astype(jnp.bfloat16)
    grad_up = jnp.einsum(
        "rf,rd->fd", d_up_act, input_rows, preferred_element_type=jnp.float32
    ).astype(jnp.bfloat16)
    partial_sum = jnp.einsum("rf,fd->rd", d_gate_act, gate_w, preferred_element_type=jnp.float32)
    partial_sum = partial_sum + jnp.einsum(
        "rf,fd->rd", d_up_act, up_w, preferred_element_type=jnp.float32
    )
    rounded = partial_sum.astype(jnp.bfloat16).reshape(experts, groups, capacity, features)
    held = lax.optimization_barrier(rounded).astype(jnp.float32)
    slot_total = lax.psum_scatter(
        held.astype(jnp.bfloat16), "dp", scatter_dimension=1, tiled=True
    ).astype(jnp.float32)
    returned = lax.all_to_all(
        slot_total[:, 0].astype(jnp.bfloat16), "expert", split_axis=0, concat_axis=0, tiled=True
    ).astype(jnp.float32)
    summed = jnp.einsum(
        "tec,ecd->td", own_place.astype(jnp.float32), returned, precision=lax.Precision.HIGHEST
    )
    return (summed.astype(jnp.bfloat16), grad_gate[None], grad_up[None], grad_down[None])


def solution(mesh):
    in_specs = (
        P(("dp", "expert"), None),
        P(("dp", "expert"), None),
        P(("dp", "expert"), None),
        P(("dp", "expert"), None),
        P("expert", "dp", None),
        P("expert", "dp", None),
        P("expert", "dp", None),
    )
    out_specs = (
        P(("dp", "expert"), None),
        P("expert", "dp", None),
        P("expert", "dp", None),
        P("expert", "dp", None),
    )
    return jax.shard_map(
        per_device, mesh=mesh, in_specs=in_specs, out_specs=out_specs, check_vma=False
    )
```

profile of v0, /device:TPU:1, one launch (start us, length us, event | category | flops | bytes accessed | tf_op | source)
XLA Modules:
  0.0 475.0 jit_solution(9894178153079241439)
XLA Ops:
  7.2 0.9 copy.53
  8.3 0.5 select_reduce_fusion.1
  9.2 1.7 convolution_convert_fusion
  10.9 1.6 copy.63
  12.5 64.0 %all_to_all.15 = bf16[64,4,4096]{2,1,0:T(4,128)(2,1)S(1)} all-to-all(bf16[64,4,4096]{2,1,0:T(4,128)(2,1)S(1)} %copy.63), channel_id=1, replica_groups=mesh['dp'=4,'expert'=64] {'expert'}, dimensions={0} | all-to-all | bytes 4194304 | tf_op jit(solution)/shard_map/all_to_all | solution.py:47
  76.6 2.5 copy.64
  79.1 0.6 copy-done.7
  79.8 0.1 select_reduce_fusion
  80.1 1.8 convolution_convert_fusion.1
  81.9 1.6 copy.59
  83.5 56.9 %all_to_all.16 = bf16[64,4,4096]{2,1,0:T(4,128)(2,1)S(1)} all-to-all(bf16[64,4,4096]{2,1,0:T(4,128)(2,1)S(1)} %copy.59), channel_id=1, replica_groups=mesh['dp'=4,'expert'=64] {'expert'}, dimensions={0} | all-to-all | bytes 4194304 | tf_op jit(solution)/shard_map/all_to_all | solution.py:48
  140.3 2.5 copy.60
  142.9 0.2 reduce-scatter.2.cloned.1.call-start
  143.1 18.4 %all-gather.7.cloned.1.call-done = bf16[64,16,4096]{2,0,1:T(8,128)(2,1)} async-done(((bf16[64,4,4096]{2,0,1:T(8,128)(2,1)}), bf16[64,16,4096]{2,0,1:T(8,128)(2,1)}) %all-gather.7.cloned.1.call-update) | async-done | bytes 8388624 | tf_op jit(solution)/shard_map/all_gather | solution.py:53
  161.5 11.2 %copy.65 = bf16[64,16,4096]{2,1,0:T(8,128)(2,1)} copy(bf16[64,16,4096]{2,0,1:T(8,128)(2,1)} %all-gather.7.cloned.1.call-done) | data formatting | bytes 16777216 | tf_op jit(solution)/shard_map/all_gather | solution.py:53
  172.8 7.5 %fusion.7 = f32[1024,192]{0,1:T(8,128)} fusion(bf16[1024,4096]{1,0:T(8,128)(2,1)} %bitcast.48, bf16[1,192,4096]{2,1,0:T(8,128)(2,1)S(1)} %copy-done), kind=kOutput, calls=%fused_computation.14 | convolution fusion | flops 1610612736 | bytes 10747904 | tf_op jit(solution)/shard_map/rd,fd->rf/dot_general | solution.py:61
  180.3 3.8 fusion.10
  184.2 65.9 %all-gather.5.cloned.1.call-done = bf16[64,16,4096]{2,0,1:T(8,128)(2,1)} async-done(((bf16[64,4,4096]{2,0,1:T(8,128)(2,1)}), bf16[64,16,4096]{2,0,1:T(8,128)(2,1)}) %all-gather.5.cloned.1.call-update) | async-done | bytes 8388624 | tf_op jit(solution)/shard_map/all_gather | solution.py:54
  250.1 11.6 %copy.61 = bf16[64,16,4096]{2,1,0:T(8,128)(2,1)} copy(bf16[64,16,4096]{2,0,1:T(8,128)(2,1)} %all-gather.5.cloned.1.call-done) | data formatting | bytes 16777216 | tf_op jit(solution)/shard_map/all_gather | solution.py:54
  261.6 6.4 %multiply_convert_fusion.1 = (bf16[1024,192]{0,1:T(8,128)(2,1)S(1)}, bf16[1024,192]{0,1:T(8,128)(2,1)S(1)}) fusion(f32[1024,192]{0,1:T(8,128)S(1)} %copy-done.9, f32[1024,192]{0,1:T(8,128)S(1)} %copy-done.11, bf16[1024,4096]{1,0:T(8,128)(2,1)} %bitcast.52, bf16[1,192,4096]{2,1,0:T(8,128)(2,1)S(1)} %copy-done.8), kind=kOutput, calls=%fused_computation.22 | convolution fusion | flops 1613168640 | bytes 12320768 | tf_op jit(solution)/shard_map/rd,fd->rf/dot_general | solution.py:66
  268.1 8.1 %fusion.5 = f32[1024,4096]{1,0:T(8,128)} fusion(bf16[1024,192]{0,1:T(8,128)(2,1)S(1)} %get-tuple-element.5, bf16[1,192,4096]{2,1,0:T(8,128)(2,1)S(1)} %copy-done), kind=kOutput, calls=%fused_computation.12 | convolution fusion | flops 1610612736 | bytes 18743296 | tf_op jit(solution)/shard_map/rf,fd->rd/dot_general | solution.py:80
  276.2 11.4 %add_convert_fusion = bf16[1024,4096]{1,0:T(8,128)(2,1)} fusion(f32[1024,4096]{1,0:T(8,128)} %fusion.5, bf16[1024,192]{0,1:T(8,128)(2,1)S(1)} %get-tuple-element.4, bf16[1,192,4096]{2,1,0:T(8,128)(2,1)S(1)} %copy-done.3), kind=kOutput, calls=%fused_computation | convolution fusion | flops 1619001344 | bytes 27131904 | tf_op jit(solution)/shard_map/rf,fd->rd/dot_general | solution.py:81
  287.6 13.3 %reshape.48 = bf16[64,4,4,4096]{3,2,1,0:T(4,128)(2,1)} reshape(bf16[1024,4096]{1,0:T(8,128)(2,1)} %add_convert_fusion) | data formatting | bytes 16777216 | tf_op jit(solution)/shard_map/reshape | solution.py:84
  300.9 11.2 %copy.66 = bf16[64,4,4,4096]{3,0,2,1:T(8,128)(2,1)} copy(bf16[64,4,4,4096]{3,2,1,0:T(4,128)(2,1)} %reshape.48) | data formatting | bytes 16777216 | tf_op jit(solution)/shard_map/optimization_barrier | solution.py:85
  312.1 84.3 %reduce-scatter.2.cloned.1.call-done = bf16[64,1,4,4096]{3,0,2,1:T(8,128)(2,1)} async-done(((bf16[64,4,4,4096]{3,0,2,1:T(8,128)(2,1)}), bf16[64,1,4,4096]{3,0,2,1:T(8,128)(2,1)}) %reduce-scatter.2.cloned.1.call-update) | async-done | bytes 2097168 | tf_op jit(solution)/shard_map/reduce_scatter | solution.py:86
  396.4 4.6 copy.67
  401.0 11.4 %all-to-all-start.2 = ((bf16[64,4,4096]{2,1,0:T(4,128)(2,1)}), bf16[64,4,4096]{2,1,0:T(4,128)(2,1)}, u32[]{:S(2)}, u32[]{:S(2)}) async-start(bf16[64,4,4096]{2,1,0:T(4,128)(2,1)} %copy.67), calls=%async_computation.3 | async-start | bytes 4194304 | tf_op jit(solution)/shard_map/all_to_all | solution.py:89
  412.4 6.3 %fusion.1 = bf16[1,192,4096]{2,1,0:T(8,128)(2,1)} fusion(bf16[1024,192]{0,1:T(8,128)(2,1)S(1)} %copy-done.5, bf16[1024,4096]{1,0:T(8,128)(2,1)} %bitcast.49), kind=kOutput, calls=%fused_computation.7 | convolution fusion | flops 1611399168 | bytes 10354688 | tf_op jit(solution)/shard_map/rf,rd->fd/dot_general | solution.py:77
  418.7 6.4 %fusion = bf16[1,192,4096]{2,1,0:T(8,128)(2,1)} fusion(bf16[1024,192]{0,1:T(8,128)(2,1)S(1)} %get-tuple-element.5, bf16[1024,4096]{1,0:T(8,128)(2,1)} %bitcast.50), kind=kOutput, calls=%fused_computation.6 | convolution fusion | flops 1611399168 | bytes 10354688 | tf_op jit(solution)/shard_map/rf,rd->fd/dot_general | solution.py:74
  425.2 6.5 %fusion.2 = bf16[1,192,4096]{2,1,0:T(8,128)(2,1)} fusion(bf16[1024,4096]{1,0:T(8,128)(2,1)} %bitcast.53, f32[1024,192]{0,1:T(8,128)S(1)} %copy-done.12, f32[1024,192]{0,1:T(8,128)S(1)} %copy-done.10), kind=kOutput, calls=%fused_computation.8 | convolution fusion | flops 1612578816 | bytes 11534336 | tf_op jit(solution)/shard_map/rf,rd->fd/dot_general | solution.py:71
  431.7 31.7 %all-to-all-done.2 = bf16[64,4,4096]{2,1,0:T(4,128)(2,1)} async-done(((bf16[64,4,4096]{2,1,0:T(4,128)(2,1)}), bf16[64,4,4096]{2,1,0:T(4,128)(2,1)}, u32[]{:S(2)}, u32[]{:S(2)}) %all-to-all-start.2) | async-done | bytes 2097184 | tf_op jit(solution)/shard_map/all_to_all | solution.py:89
  463.4 4.6 fusion.3
  (39 shorter events, 0.9 us)
Async XLA Ops:
  7.2 165.6 %copy-start = (bf16[1,192,4096]{2,1,0:T(8,128)(2,1)S(1)}, bf16[1,192,4096]{2,1,0:T(8,128)(2,1)}, u32[]{:S(2)}) copy-start(bf16[1,192,4096]{2,1,0:T(8,128)(2,1)} %param.11) | copy-start | bytes 4718596
  7.2 154.4 %all-gather.7.cloned.1.call-start = ((), (), s32[]{:S(2)}) async-start(), calls=%async_computation.6 | async-start | bytes 10485760 | tf_op jit(solution)/shard_map/all_gather | solution.py:53
  79.1 0.7 copy-start.7
  79.1 1.0 copy-start.6
  79.1 171.0 %all-gather.5.cloned.1.call-start = ((), (), s32[]{:S(2)}) async-start(), calls=%async_computation.5 | async-start | bytes 10485760 | tf_op jit(solution)/shard_map/all_gather | solution.py:54
  142.9 253.6 %reduce-scatter.2.cloned.1.call-start = ((), (), s32[]{:S(2)}) async-start(), calls=%async_computation.4 | async-start | bytes 10485760 | tf_op jit(solution)/shard_map/reduce_scatter | solution.py:86
  172.8 7.5 %copy-start.2 = (bf16[64,16,4096]{2,1,0:T(8,128)(2,1)S(1)}, bf16[64,16,4096]{2,1,0:T(8,128)(2,1)}, u32[]{:S(2)}) copy-start(bf16[64,16,4096]{2,1,0:T(8,128)(2,1)} %copy.65) | copy-start | bytes 25165828
  172.8 7.6 %copy-start.3 = (bf16[1,192,4096]{2,1,0:T(8,128)(2,1)S(1)}, bf16[1,192,4096]{2,1,0:T(8,128)(2,1)}, u32[]{:S(2)}) copy-start(bf16[1,192,4096]{2,1,0:T(8,128)(2,1)} %param.12) | copy-start | bytes 4718596
  250.1 11.6 %copy-start.8 = (bf16[1,192,4096]{2,1,0:T(8,128)(2,1)S(1)}, bf16[1,192,4096]{2,1,0:T(8,128)(2,1)}, u32[]{:S(2)}) copy-start(bf16[1,192,4096]{2,1,0:T(8,128)(2,1)} %param.13) | copy-start | bytes 4718596
  250.1 11.6 %copy-start.9 = (f32[1024,192]{0,1:T(8,128)S(1)}, f32[1024,192]{0,1:T(8,128)}, u32[]{:S(2)}) copy-start(f32[1024,192]{0,1:T(8,128)} %fusion.7) | copy-start | bytes 2359300
  250.1 11.6 %copy-start.11 = (f32[1024,192]{0,1:T(8,128)S(1)}, f32[1024,192]{0,1:T(8,128)}, u32[]{:S(2)}) copy-start(f32[1024,192]{0,1:T(8,128)} %fusion.10) | copy-start | bytes 2359300
  268.1 8.1 %copy-start.4 = (bf16[1024,192]{0,1:T(8,128)(2,1)}, bf16[1024,192]{0,1:T(8,128)(2,1)S(1)}, u32[]{:S(2)}) copy-start(bf16[1024,192]{0,1:T(8,128)(2,1)S(1)} %get-tuple-element.4) | copy-start | bytes 1179652
  401.0 11.4 %copy-start.5 = (bf16[1024,192]{0,1:T(8,128)(2,1)S(1)}, bf16[1024,192]{0,1:T(8,128)(2,1)}, u32[]{:S(2)}) copy-start(bf16[1024,192]{0,1:T(8,128)(2,1)} %copy-done.4) | copy-start | bytes 1179652
  401.0 62.4 %all-to-all-start.2 = ((bf16[64,4,4096]{2,1,0:T(4,128)(2,1)}), bf16[64,4,4096]{2,1,0:T(4,128)(2,1)}, u32[]{:S(2)}, u32[]{:S(2)}) async-start(bf16[64,4,4096]{2,1,0:T(4,128)(2,1)} %copy.67), calls=%async_computation.3 | async-start | bytes 4194304 | tf_op jit(solution)/shard_map/all_to_all | solution.py:89
  418.7 6.5 %copy-start.10 = (f32[1024,192]{0,1:T(8,128)S(1)}, f32[1024,192]{0,1:T(8,128)}, u32[]{:S(2)}) copy-start(f32[1024,192]{0,1:T(8,128)} %fusion.7) | copy-start | bytes 2359300
  418.7 6.5 %copy-start.12 = (f32[1024,192]{0,1:T(8,128)S(1)}, f32[1024,192]{0,1:T(8,128)}, u32[]{:S(2)}) copy-start(f32[1024,192]{0,1:T(8,128)} %fusion.10) | copy-start | bytes 2359300
  425.2 42.8 %copy-start.1 = (bf16[1,192,4096]{2,1,0:T(8,128)(2,1)S(1)}, bf16[1,192,4096]{2,1,0:T(8,128)(2,1)}, u32[]{:S(2)}) copy-start(bf16[1,192,4096]{2,1,0:T(8,128)(2,1)} %param.11) | copy-start | bytes 4718596
Sparse Core Ops, SparseCore 0:
  79.2 82.2 all-gather.6
  163.4 86.6 all-gather.4
  312.3 84.1 reduce-scatter.1
where the time goes:
time: 484 us; the launch traced here: 475 us
  waiting for transfers between devices  200 us (41%)
  blocking collectives  121 us (25%)
  matrix products  64.6 us (13%)
  local copies, waits for them, and re-layouts  62.1 us (13%)
  between operations  14.4 us (3%)
  starting transfers between devices  11.7 us (2%)
    reduce_scatter x1, waiting for transfers between devices, per_device(): lax.psum_scatter(held.astype(jnp.bfloat16), 'dp', scatter_dimension=1, ti...  84.3 us
    all_gather x1, waiting for transfers between devices, per_device(): lax.all_gather(grad_recv, 'dp', axis=1, tiled=True)  65.9 us
    all_to_all x1, blocking collectives, per_device(): lax.all_to_all(input_send, 'expert', split_axis=0, concat_axis=0, tiled=T...  64 us
    all_to_all x1, blocking collectives, per_device(): lax.all_to_all(grad_send, 'expert', split_axis=0, concat_axis=0, tiled=True)  56.9 us
    all_to_all x1, waiting for transfers between devices, per_device(): lax.all_to_all(slot_total[:, 0].astype(jnp.bfloat16), 'expert', split_axi...  31.7 us
    all_gather x1, waiting for transfers between devices, per_device(): lax.all_gather(input_recv, 'dp', axis=1, tiled=True)  18.4 us
    reshape x1, local copies, waits for them, and re-layouts, per_device(): partial_sum.astype(jnp.bfloat16)  13.3 us
    all_gather x1, local copies, waits for them, and re-layouts, per_device(): lax.all_gather(grad_recv, 'dp', axis=1, tiled=True)  11.6 us
  transfers between devices with their start and end apart: 4, of which 4 were waited for; matrix products, arithmetic and copies ran while one was open for 10% of the time, Pallas kernels for 0%

commit v1 on v0

--- a/solution.py
+++ b/solution.py
@@ -50,7 +50,9 @@
     input_recv = input_recv.reshape(experts, 1, capacity, features)
     grad_recv = grad_recv.reshape(experts, 1, capacity, features)
     input_slots, grad_slots = (
-        lax.all_gather(input_recv, "dp", axis=1, tiled=True),
+        jnp.concatenate(
+            lax.all_to_all(jnp.stack([input_recv] * lax.axis_size("dp")), "dp", 0, 0), axis=1
+        ),
         lax.all_gather(grad_recv, "dp", axis=1, tiled=True),
     )
     input_rows = input_slots.reshape(-1, features)

time: 484 us -> 516 us (1.066)
  blocking collectives: 121 us -> 223 us
  waiting for transfers between devices: 200 us -> 119 us
  local copies, waits for them, and re-layouts: 62.1 us -> 76.5 us
    all_to_all x0 -> x1, blocking collectives: none -> 102 us  [per_device(): lax.all_to_all(jnp.stack([input_recv] * lax.axis_size('dp')), 'dp', 0, 0)]
    all_gather x1, waiting for transfers between devices: 65.9 us -> 0.01 us  [per_device(): lax.all_gather(grad_recv, 'dp', axis=1, tiled=True)]
    another operation x0 -> x2, local copies, waits for them, and re-layouts: none -> 21.9 us  [the longest x1 12.5 us: per_device(): input_rows = input_slots.reshape(-1, features)]
    all_gather x1 -> x0, waiting for transfers between devices: 18.4 us -> none  [per_device(): lax.all_gather(input_recv, 'dp', axis=1, tiled=True)]
    all_gather x1 -> x0, local copies, waits for them, and re-layouts: 11.2 us -> none  [per_device(): lax.all_gather(input_recv, 'dp', axis=1, tiled=True)]
    all_to_all x1, blocking collectives: 56.9 us -> 64 us  [per_device(): lax.all_to_all(grad_send, 'expert', split_axis=0, concat_axis=0, tiled=True)]
    all_to_all x1, blocking collectives: 64 us -> 57.2 us  [per_device(): lax.all_to_all(input_send, 'expert', split_axis=0, concat_axis=0, tiled=T...]
    reshape x0 -> x1, local copies, waits for them, and re-layouts: none -> 6.17 us  [per_device(): jnp.concatenate(lax.all_to_all(jnp.stack([input_recv] * lax.axis_size('dp...]
  transfers between devices with their start and end apart: 4 -> 3, of which waited for: 4 -> 2; matrix products, arithmetic and copies ran while one was open for 10% -> 11% of each run, Pallas kernels for 0% -> 0%
where the time goes in v1:
time: 516 us; the launch traced here: 507 us
  blocking collectives  223 us (43%)
  waiting for transfers between devices  119 us (23%)
  local copies, waits for them, and re-layouts  76.5 us (15%)
  matrix products  61.2 us (12%)
  between operations  14.6 us (3%)
  starting transfers between devices  11.4 us (2%)
    all_to_all x1, blocking collectives, per_device(): lax.all_to_all(jnp.stack([input_recv] * lax.axis_size('dp')), 'dp', 0, 0)  102 us
    reduce_scatter x1, waiting for transfers between devices, per_device(): lax.psum_scatter(held.astype(jnp.bfloat16), 'dp', scatter_dimension=1, ti...  84.4 us
    all_to_all x1, blocking collectives, per_device(): lax.all_to_all(grad_send, 'expert', split_axis=0, concat_axis=0, tiled=True)  64 us
    all_to_all x1, blocking collectives, per_device(): lax.all_to_all(input_send, 'expert', split_axis=0, concat_axis=0, tiled=T...  57.2 us
    all_to_all x1, waiting for transfers between devices, per_device(): lax.all_to_all(slot_total[:, 0].astype(jnp.bfloat16), 'expert', split_axi...  35 us
    reshape x1, local copies, waits for them, and re-layouts, per_device(): partial_sum.astype(jnp.bfloat16)  13.1 us
    another operation x1, local copies, waits for them, and re-layouts, per_device(): input_rows = input_slots.reshape(-1, features)  12.5 us
    dot_general x1, matrix products, per_device(): jnp.einsum('rf,fd->rd', d_up_act, up_w, preferred_element_type=jnp.float32)  11.4 us
  transfers between devices with their start and end apart: 3, of which 2 were waited for; matrix products, arithmetic and copies ran while one was open for 11% of the time, Pallas kernels for 0%

profile of v1, /device:TPU:1, one launch (start us, length us, event | category | flops | bytes accessed | tf_op | source)
XLA Modules:
  0.0 507.5 jit_solution(4563966732281106380)
XLA Ops:
  7.2 0.9 copy.52
  8.3 0.5 select_reduce_fusion.1
  8.8 0.8 copy.55
  9.6 0.1 select_reduce_fusion
  9.8 2.7 convolution_convert_fusion.1
  12.5 1.6 copy.58
  14.2 64.0 %all_to_all.20 = bf16[64,4,4096]{2,1,0:T(4,128)(2,1)S(1)} all-to-all(bf16[64,4,4096]{2,1,0:T(4,128)(2,1)S(1)} %copy.58), channel_id=1, replica_groups=mesh['dp'=4,'expert'=64] {'expert'}, dimensions={0} | all-to-all | bytes 4194304 | tf_op jit(solution)/shard_map/all_to_all | solution.py:48
  78.2 2.5 copy.59
  81.2 0.5 copy-done.6
  81.6 0.7 convolution_convert_fusion
  82.4 1.6 copy.62
  84.0 57.2 %all_to_all.21 = bf16[64,4,4096]{2,1,0:T(4,128)(2,1)} all-to-all(bf16[64,4,4096]{2,1,0:T(4,128)(2,1)S(1)} %copy.62), channel_id=1, replica_groups=mesh['dp'=4,'expert'=64] {'expert'}, dimensions={0} | all-to-all | bytes 4194304 | tf_op jit(solution)/shard_map/all_to_all | solution.py:47
  141.2 9.4 %stack.3 = bf16[4,64,1,4,4096]{4,3,1,2,0:T(4,128)(2,1)} broadcast(bf16[64,4,4096]{2,1,0:T(4,128)(2,1)} %all_to_all.21), dimensions={1,3,4} | broadcast | bytes 10485760 | tf_op jit(solution)/shard_map/stack | solution.py:54
  150.6 102.0 %all_to_all.22 = bf16[4,64,1,4,4096]{4,3,1,2,0:T(4,128)(2,1)S(1)} all-to-all(bf16[4,64,1,4,4096]{4,3,1,2,0:T(4,128)(2,1)} %stack.3), channel_id=1, replica_groups=mesh['dp'=4,'expert'=64] {'dp'}, dimensions={0} | all-to-all | bytes 16777216 | tf_op jit(solution)/shard_map/all_to_all | solution.py:54
  252.6 6.2 %copy.63 = bf16[64,4,1,4,4096]{4,3,1,0,2:T(4,128)(2,1)} copy(bf16[64,4,1,4,4096]{4,3,0,2,1:T(4,128)(2,1)S(1)} %bitcast.50) | data formatting | bytes 16777216 | tf_op jit(solution)/shard_map/reshape | solution.py:53
  258.8 12.5 %reshape_reshape.3 = bf16[1024,4096]{1,0:T(8,128)(2,1)} reshape(bf16[64,4,1,4,4096]{4,3,1,0,2:T(4,128)(2,1)} %copy.63) | data formatting | bytes 16777216 | tf_op jit(solution)/shard_map/reshape;reshape | solution.py:58
  271.3 7.3 %fusion.7 = f32[1024,192]{0,1:T(8,128)} fusion(bf16[1024,4096]{1,0:T(8,128)(2,1)} %reshape_reshape.3, bf16[1,192,4096]{2,1,0:T(8,128)(2,1)S(1)} %copy-done), kind=kOutput, calls=%fused_computation.14 | convolution fusion | flops 1610612736 | bytes 10747904 | tf_op jit(solution)/shard_map/rd,fd->rf/dot_general | solution.py:63
  278.6 3.8 fusion.10
  282.4 11.3 %copy.60 = bf16[64,16,4096]{2,1,0:T(8,128)(2,1)} copy(bf16[64,16,4096]{2,0,1:T(8,128)(2,1)} %all-gather.3.cloned.1.call-done) | data formatting | bytes 16777216 | tf_op jit(solution)/shard_map/all_gather | solution.py:56
  293.8 6.4 %multiply_convert_fusion.1 = (bf16[1024,192]{0,1:T(8,128)(2,1)S(1)}, bf16[1024,192]{0,1:T(8,128)(2,1)S(1)}) fusion(f32[1024,192]{0,1:T(8,128)S(1)} %copy-done.8, f32[1024,192]{0,1:T(8,128)S(1)} %copy-done.10, bf16[1024,4096]{1,0:T(8,128)(2,1)} %bitcast.51, bf16[1,192,4096]{2,1,0:T(8,128)(2,1)S(1)} %copy-done.7), kind=kOutput, calls=%fused_computation.22 | convolution fusion | flops 1613168640 | bytes 12320768 | tf_op jit(solution)/shard_map/rd,fd->rf/dot_general | solution.py:68
  300.3 8.4 %fusion.5 = f32[1024,4096]{1,0:T(8,128)} fusion(bf16[1024,192]{0,1:T(8,128)(2,1)S(1)} %get-tuple-element.5, bf16[1,192,4096]{2,1,0:T(8,128)(2,1)S(1)} %copy-done), kind=kOutput, calls=%fused_computation.12 | convolution fusion | flops 1610612736 | bytes 18743296 | tf_op jit(solution)/shard_map/rf,fd->rd/dot_general | solution.py:82
  308.6 11.4 %add_convert_fusion = bf16[1024,4096]{1,0:T(8,128)(2,1)} fusion(f32[1024,4096]{1,0:T(8,128)} %fusion.5, bf16[1024,192]{0,1:T(8,128)(2,1)S(1)} %get-tuple-element.4, bf16[1,192,4096]{2,1,0:T(8,128)(2,1)S(1)} %copy-done.3), kind=kOutput, calls=%fused_computation | convolution fusion | flops 1619001344 | bytes 27131904 | tf_op jit(solution)/shard_map/rf,fd->rd/dot_general | solution.py:83
  320.0 13.1 %reshape.46 = bf16[64,4,4,4096]{3,2,1,0:T(4,128)(2,1)} reshape(bf16[1024,4096]{1,0:T(8,128)(2,1)} %add_convert_fusion) | data formatting | bytes 16777216 | tf_op jit(solution)/shard_map/reshape | solution.py:86
  333.1 11.2 %copy.64 = bf16[64,4,4,4096]{3,0,2,1:T(8,128)(2,1)} copy(bf16[64,4,4,4096]{3,2,1,0:T(4,128)(2,1)} %reshape.46) | data formatting | bytes 16777216 | tf_op jit(solution)/shard_map/optimization_barrier | solution.py:87
  344.3 84.4 %reduce-scatter.2.cloned.1.call-done = bf16[64,1,4,4096]{3,0,2,1:T(8,128)(2,1)} async-done(((bf16[64,4,4,4096]{3,0,2,1:T(8,128)(2,1)}), bf16[64,1,4,4096]{3,0,2,1:T(8,128)(2,1)}) %reduce-scatter.2.cloned.1.call-update) | async-done | bytes 2097168 | tf_op jit(solution)/shard_map/reduce_scatter | solution.py:88
  428.7 4.6 copy.65
  433.3 11.3 %all-to-all-start.3 = ((bf16[64,4,4096]{2,1,0:T(4,128)(2,1)}), bf16[64,4,4096]{2,1,0:T(4,128)(2,1)}, u32[]{:S(2)}, u32[]{:S(2)}) async-start(bf16[64,4,4096]{2,1,0:T(4,128)(2,1)} %copy.65), calls=%async_computation.4 | async-start | bytes 4194304 | tf_op jit(solution)/shard_map/all_to_all | solution.py:91
  444.6 6.5 %fusion.1 = bf16[1,192,4096]{2,1,0:T(8,128)(2,1)} fusion(bf16[1024,192]{0,1:T(8,128)(2,1)S(1)} %copy-done.5, bf16[1024,4096]{1,0:T(8,128)(2,1)} %reshape_reshape.3), kind=kOutput, calls=%fused_computation.7 | convolution fusion | flops 1611399168 | bytes 10354688 | tf_op jit(solution)/shard_map/rf,rd->fd/dot_general | solution.py:79
  451.1 6.5 %fusion = bf16[1,192,4096]{2,1,0:T(8,128)(2,1)} fusion(bf16[1024,192]{0,1:T(8,128)(2,1)S(1)} %get-tuple-element.5, bf16[1024,4096]{1,0:T(8,128)(2,1)} %reshape_reshape.3), kind=kOutput, calls=%fused_computation.6 | convolution fusion | flops 1611399168 | bytes 10354688 | tf_op jit(solution)/shard_map/rf,rd->fd/dot_general | solution.py:76
  457.6 3.0 fusion.2
  460.6 35.0 %all-to-all-done.3 = bf16[64,4,4096]{2,1,0:T(4,128)(2,1)} async-done(((bf16[64,4,4096]{2,1,0:T(4,128)(2,1)}), bf16[64,4,4096]{2,1,0:T(4,128)(2,1)}, u32[]{:S(2)}, u32[]{:S(2)}) %all-to-all-start.3) | async-done | bytes 2097184 | tf_op jit(solution)/shard_map/all_to_all | solution.py:91
  495.6 4.6 fusion.3
  (41 shorter events, 0.8 us)
Async XLA Ops:
  7.2 264.1 %copy-start = (bf16[1,192,4096]{2,1,0:T(8,128)(2,1)S(1)}, bf16[1,192,4096]{2,1,0:T(8,128)(2,1)}, u32[]{:S(2)}) copy-start(bf16[1,192,4096]{2,1,0:T(8,128)(2,1)} %param.11) | copy-start | bytes 4718596
  7.2 275.3 %all-gather.3.cloned.1.call-start = ((), (), s32[]{:S(2)}) async-start(), calls=%async_computation.6 | async-start | bytes 10485760 | tf_op jit(solution)/shard_map/all_gather | solution.py:56
  80.7 0.9 copy-start.6
  80.7 348.0 %reduce-scatter.2.cloned.1.call-start = ((), (), s32[]{:S(2)}) async-start(), calls=%async_computation.5 | async-start | bytes 10485760 | tf_op jit(solution)/shard_map/reduce_scatter | solution.py:88
  271.3 7.3 %copy-start.2 = (bf16[1024,4096]{1,0:T(8,128)(2,1)S(1)}, bf16[1024,4096]{1,0:T(8,128)(2,1)}, u32[]{:S(2)}) copy-start(bf16[1024,4096]{1,0:T(8,128)(2,1)} %reshape_reshape.3) | copy-start | bytes 25165828
  271.3 7.3 %copy-start.3 = (bf16[1,192,4096]{2,1,0:T(8,128)(2,1)S(1)}, bf16[1,192,4096]{2,1,0:T(8,128)(2,1)}, u32[]{:S(2)}) copy-start(bf16[1,192,4096]{2,1,0:T(8,128)(2,1)} %param.12) | copy-start | bytes 4718596
  282.4 11.4 %copy-start.7 = (bf16[1,192,4096]{2,1,0:T(8,128)(2,1)S(1)}, bf16[1,192,4096]{2,1,0:T(8,128)(2,1)}, u32[]{:S(2)}) copy-start(bf16[1,192,4096]{2,1,0:T(8,128)(2,1)} %param.13) | copy-start | bytes 4718596
  282.4 11.4 %copy-start.8 = (f32[1024,192]{0,1:T(8,128)S(1)}, f32[1024,192]{0,1:T(8,128)}, u32[]{:S(2)}) copy-start(f32[1024,192]{0,1:T(8,128)} %fusion.7) | copy-start | bytes 2359300
  282.4 11.4 %copy-start.10 = (f32[1024,192]{0,1:T(8,128)S(1)}, f32[1024,192]{0,1:T(8,128)}, u32[]{:S(2)}) copy-start(f32[1024,192]{0,1:T(8,128)} %fusion.10) | copy-start | bytes 2359300
  300.3 8.4 %copy-start.4 = (bf16[1024,192]{0,1:T(8,128)(2,1)}, bf16[1024,192]{0,1:T(8,128)(2,1)S(1)}, u32[]{:S(2)}) copy-start(bf16[1024,192]{0,1:T(8,128)(2,1)S(1)} %get-tuple-element.4) | copy-start | bytes 1179652
  433.3 11.4 %copy-start.5 = (bf16[1024,192]{0,1:T(8,128)(2,1)S(1)}, bf16[1024,192]{0,1:T(8,128)(2,1)}, u32[]{:S(2)}) copy-start(bf16[1024,192]{0,1:T(8,128)(2,1)} %copy-done.4) | copy-start | bytes 1179652
  433.3 62.4 %all-to-all-start.3 = ((bf16[64,4,4096]{2,1,0:T(4,128)(2,1)}), bf16[64,4,4096]{2,1,0:T(4,128)(2,1)}, u32[]{:S(2)}, u32[]{:S(2)}) async-start(bf16[64,4,4096]{2,1,0:T(4,128)(2,1)} %copy.65), calls=%async_computation.4 | async-start | bytes 4194304 | tf_op jit(solution)/shard_map/all_to_all | solution.py:91
  444.6 13.0 %slice-start = ((s8[8388608]{0:T(1024)(128)(4,1)}), s8[4194304]{0:T(1024)(128)(4,1)S(1)}, s32[]{:S(2)}) async-start(s8[8388608]{0:T(1024)(128)(4,1)} %bitcast.52), calls=%async_computation.7 | async-start | bytes 8388608
  451.1 6.5 %slice-start.1 = ((s8[8388608]{0:T(1024)(128)(4,1)}), s8[4194304]{0:T(1024)(128)(4,1)S(1)}, s32[]{:S(2)}) async-start(s8[8388608]{0:T(1024)(128)(4,1)} %bitcast.52), calls=%async_computation.8 | async-start | bytes 8388608
  451.1 6.5 %copy-start.9 = (f32[1024,192]{0,1:T(8,128)S(1)}, f32[1024,192]{0,1:T(8,128)}, u32[]{:S(2)}) copy-start(f32[1024,192]{0,1:T(8,128)} %fusion.7) | copy-start | bytes 2359300
  451.1 6.5 %copy-start.11 = (f32[1024,192]{0,1:T(8,128)S(1)}, f32[1024,192]{0,1:T(8,128)}, u32[]{:S(2)}) copy-start(f32[1024,192]{0,1:T(8,128)} %fusion.10) | copy-start | bytes 2359300
  457.6 42.6 %copy-start.1 = (bf16[1,192,4096]{2,1,0:T(8,128)(2,1)S(1)}, bf16[1,192,4096]{2,1,0:T(8,128)(2,1)}, u32[]{:S(2)}) copy-start(bf16[1,192,4096]{2,1,0:T(8,128)(2,1)} %param.11) | copy-start | bytes 4718596
Sparse Core Ops, SparseCore 0:
  80.9 88.6 all-gather.2
  344.4 84.2 reduce-scatter.1
